TPU v7x, 32 devices: a whole 2x2x4 slice. The times are simulated.
32 devices in a mesh: row: 16 (over z, x, core), grp: 2 (over y).
Axes of the slice: x: 2, y: 2, z: 4, core: 2. Of those that a mesh axis runs over, the one named last changes fastest.
Arguments:
- panel_rows: bfloat16 [16384, 1024], P(('row', 'grp')), may hold values from -300 to 300, as said below
- sign_bits: int32 [16384], P(('row', 'grp')), may hold values from 0 to 1
- sample_rows: int32 [8192], replicated, may hold values from 0 to 16383, as said below
Outputs:
- factor: float32 [1024, 1024], P('row', 'grp')
Inputs may be any that keep to these rules, and one draw needn't show every extreme that they name: `sample_rows`: distinct and ascending. Each aligned block of 512 rows (the rows of one device) holds at most 512 sampled rows, and at least a quarter of these blocks hold exactly 512. `panel_rows`: finite values.
All inputs are finite; a program needn't handle non-finite values.
Results may differ from a plain program's by a relative error of at most 0.0011.
Values may be sent and summed in bfloat16 or wider, within the bound.
No kernel may reach another device: no remote copies, remote signals or barrier semaphores. Data moves between devices by JAX's collectives and lax.ppermute only.
A program may use at most 64 MiB of HBM per device.

v0:
```python
import math
import jax
import jax.numpy as jnp
from jax import lax
from jax.sharding import PartitionSpec as P


def hadamard(table_size, dtype):
    row_ids = lax.broadcasted_iota(jnp.int32, (table_size, table_size), 0)
    col_ids = lax.broadcasted_iota(jnp.int32, (table_size, table_size), 1)
    shared = row_ids & col_ids
    parity = jnp.zeros((table_size, table_size), jnp.int32)
    for bit_pos in range(table_size.bit_length() - 1):
        parity = parity ^ shared >> bit_pos & 1
    return (1 - 2 * parity).astype(dtype)


def mix_lead(exchanged):
    lead_table = hadamard(exchanged.shape[0], jnp.float32)
    return jnp.einsum("ab,bic->aic", lead_table, exchanged, precision=lax.Precision.HIGHEST)


def mix_grp(exchanged):
    return lax.all_to_all(mix_lead(exchanged), "grp", split_axis=0, concat_axis=2, tiled=True)


def local(panel_rows, sign_bits, sample_rows):
    rows_dev, n_cols = panel_rows.shape
    n_row = lax.axis_size("row")
    n_grp = lax.axis_size("grp")
    flipped = panel_rows * (1 - 2 * sign_bits).astype(jnp.bfloat16)[:, None]
    local_table = hadamard(rows_dev, jnp.bfloat16)
    local_mix = jnp.dot(local_table, flipped, preferred_element_type=jnp.float32)
    grp_mixed = mix_grp(
        lax.all_to_all(local_mix[None], "grp", split_axis=2, concat_axis=0, tiled=True)
    )
    num_samples = sample_rows.shape[0]
    total_rows = rows_dev * n_row * n_grp
    norm_scale = 1.0 / math.sqrt(total_rows * num_samples)
    col_width = n_cols // n_grp
    col_start = lax.axis_index("grp") * col_width
    held = mix_lead(lax.all_to_all(grp_mixed, "row", split_axis=1, concat_axis=0, tiled=True))
    slice_width = held.shape[1]
    block_pos = lax.broadcasted_iota(jnp.int32, (n_row, slice_width), 0)
    inner_pos = lax.broadcasted_iota(jnp.int32, (n_row, slice_width), 1)
    held_ids = (
        (block_pos * n_grp + lax.axis_index("grp")) * rows_dev
        + lax.axis_index("row") * slice_width
        + inner_pos
    ).reshape(-1)
    found_pos = jnp.clip(jnp.searchsorted(sample_rows, held_ids), 0, num_samples - 1)
    is_sampled = jnp.take(sample_rows, found_pos) == held_ids
    held_flat = held.reshape(n_row * slice_width, n_cols)
    sketch_held = jnp.where(is_sampled[:, None], held_flat * norm_scale, 0.0).astype(jnp.bfloat16)
    shard_rows = lax.all_gather(sketch_held, "grp", axis=0, tiled=True)
    own_cols = lax.dynamic_slice_in_dim(shard_rows, col_start, col_width, 1)
    partial_value = lax.dot_general(
        shard_rows, own_cols, (((0,), (0,)), ((), ())), preferred_element_type=jnp.float32
    )
    gram_block = lax.psum_scatter(partial_value, "row", scatter_dimension=0, tiled=True)
    gathered = lax.all_gather(gram_block[None], ("row", "grp"), axis=0, tiled=True)
    gram_matrix = (
        gathered.reshape(n_row, n_grp, n_cols // n_row, col_width)
        .transpose(0, 2, 1, 3)
        .reshape(n_cols, n_cols)
    )
    lower_factor = jnp.linalg.cholesky(gram_matrix)
    row_width = n_cols // n_row
    return lax.dynamic_slice(
        lower_factor, (lax.axis_index("row") * row_width, col_start), (row_width, col_width)
    )


def solution(mesh):
    return jax.shard_map(
        local,
        mesh=mesh,
        in_specs=(P(("row", "grp"), None), P(("row", "grp")), P()),
        out_specs=P("row", "grp"),
        check_vma=False,
    )
```

profile of v0, /device:TPU:0, one launch (start us, length us, event | category | flops | bytes accessed | tf_op | source)
XLA Modules:
  0.0 551.8 jit_solution(12056221303512903881)
XLA Ops:
  7.2 4.2 convolution_bitcast_fusion
  11.4 4.6 copy.17
  16.0 28.9 %all_to_all.48 = f32[1,512,1024]{1,0,2:T(1,128)S(1)} all-to-all(f32[1,512,1024]{1,0,2:T(1,128)S(1)} %copy.17), channel_id=1, replica_groups=mesh['row'=16,'grp'=2] {'grp'}, dimensions={2} | all-to-all | bytes 4194304 | tf_op jit(solution)/shard_map/all_to_all | solution.py:35
  47.6 8.8 %fusion.3 = f32[2,512,512]{2,0,1:T(2,128)S(1)} fusion(f32[1,512,2,512]{3,2,1,0:T(2,128)} %copy.26), kind=kOutput, calls=%fused_computation.10 | convolution fusion | flops 12582936 | bytes 4194304 | tf_op jit(solution)/shard_map/ab,bic->aic/dot_general | solution.py:20
  58.1 3.8 all-to-all-start.1
  62.0 23.9 %all-to-all-done.1 = f32[2,512,512]{2,1,0:T(8,128)S(1)} async-done(((f32[2,512,512]{2,1,0:T(8,128)}), f32[2,512,512]{2,1,0:T(8,128)S(1)}, u32[]{:S(2)}, u32[]{:S(2)}) %all-to-all-start.1) | async-done | bytes 2097184 | tf_op jit(solution)/shard_map/all_to_all | solution.py:24
  87.7 6.1 %copy.21 = f32[1,512,1024]{2,0,1:T(1,128)} copy(f32[1,512,1024]{1,2,0:T(8,128)} %bitcast.76) | data formatting | bytes 4194304 | tf_op jit(solution)/shard_map/all_to_all | solution.py:24
  93.8 6.3 %all-to-all-start.2 = ((f32[1,512,1024]{2,0,1:T(1,128)}), f32[1,512,1024]{2,0,1:T(1,128)S(1)}, u32[]{:S(2)}, u32[]{:S(2)}) async-start(f32[1,512,1024]{2,0,1:T(1,128)} %copy.21), calls=%async_computation.2 | async-start | bytes 4194304 | tf_op jit(solution)/shard_map/all_to_all | solution.py:42
  100.7 47.4 %while.24 = (s32[]{:T(128)}, u32[512]{0:T(512)S(1)}, u32[512]{0:T(512)S(1)}, s32[8192]{0:T(1024)S(1)}, s32[16]{0:T(128)S(1)}, /*index=5*/s32[]{:T(128)}, s32[]{:T(128)}, s32[]{}) while((s32[]{:T(128)}, u32[512]{0:T(512)S(1)}, u32[512]{0:T(512)S(1)}, s32[8192]{0:T(1024)S(1)}, s32[16]{0:T(128)S(1)}, /*index=5*/s32[]{:T(128)}, ...), condition=%wide.region_1.2_spmd.clone, body=%wide.region_0.1_spmd.clone.sunk | while | flops 10756 | bytes 46253 | solution.py:51
  100.7 3.1 gather_fusion
  156.7 33.6 %all-gather.4.cloned.1.call-done = bf16[1024,1024]{1,0:T(8,128)(2,1)} async-done(((bf16[512,1024]{1,0:T(8,128)(2,1)}), bf16[1024,1024]{1,0:T(8,128)(2,1)}) %all-gather.4.cloned.1.call-update) | async-done | bytes 2097168 | tf_op jit(solution)/shard_map/all_gather | solution.py:55
  190.3 4.5 fusion.12
  194.9 61.9 %reduce-scatter.2.cloned.1.call-done = f32[64,512]{1,0:T(8,128)} async-done(((f32[1024,512]{1,0:T(8,128)}), f32[64,512]{1,0:T(8,128)}) %reduce-scatter.2.cloned.1.call-update) | async-done | bytes 131088 | tf_op jit(solution)/shard_map/reduce_scatter | solution.py:60
  256.8 63.6 %all-gather.6.cloned.1.call-done = f32[2048,512]{1,0:T(8,128)} async-done(((f32[64,512]{1,0:T(8,128)}), f32[2048,512]{1,0:T(8,128)}) %all-gather.6.cloned.1.call-update) | async-done | bytes 4194320 | tf_op jit(solution)/shard_map/all_gather | solution.py:61
  320.4 5.4 copy.24
  328.7 5.5 copy.25
  334.2 4.4 fusion.2
  340.6 11.7 %cholesky.223 = f32[128,128]{1,0:T(8,128)S(1)} custom-call(f32[128,128]{1,0:T(8,128)S(1)} %cholesky.580), custom_call_target="Cholesky" | custom-call | tf_op jit(solution)/shard_map/jit(cholesky)/cholesky | solution.py:67
  352.4 9.8 %custom-call.59 = f32[1,128,128]{1,2,0:T(8,128)S(1)} custom-call(f32[1,128,128]{2,1,0:T(8,128)S(1)} %get-tuple-element.125), custom_call_target="InvertDiagBlocksLowerTriangular" | custom-call | tf_op jit(solution)/shard_map/jit(cholesky)/cholesky | solution.py:67
  368.6 11.9 %cholesky.244 = f32[128,128]{1,0:T(8,128)S(1)} custom-call(f32[128,128]{1,0:T(8,128)S(1)} %cholesky.584), custom_call_target="Cholesky" | custom-call | tf_op jit(solution)/shard_map/jit(cholesky)/cholesky | solution.py:67
  381.2 9.8 %custom-call.60 = f32[1,128,128]{1,2,0:T(8,128)S(1)} custom-call(f32[1,128,128]{2,1,0:T(8,128)S(1)} %get-tuple-element.122), custom_call_target="InvertDiagBlocksLowerTriangular" | custom-call | tf_op jit(solution)/shard_map/jit(cholesky)/cholesky | solution.py:67
  394.3 11.7 %cholesky.468 = f32[128,128]{1,0:T(8,128)S(1)} custom-call(f32[128,128]{1,0:T(8,128)S(1)} %cholesky.589), custom_call_target="Cholesky" | custom-call | tf_op jit(solution)/shard_map/jit(cholesky)/cholesky | solution.py:67
  407.3 9.8 %custom-call.61 = f32[1,128,128]{1,2,0:T(8,128)S(1)} custom-call(f32[1,128,128]{2,1,0:T(8,128)S(1)} %get-tuple-element.119), custom_call_target="InvertDiagBlocksLowerTriangular" | custom-call | tf_op jit(solution)/shard_map/jit(cholesky)/cholesky | solution.py:67
  420.6 12.1 %cholesky.487 = f32[128,128]{1,0:T(8,128)S(1)} custom-call(f32[128,128]{1,0:T(8,128)S(1)} %cholesky.594), custom_call_target="Cholesky" | custom-call | tf_op jit(solution)/shard_map/jit(cholesky)/cholesky | solution.py:67
  434.0 9.8 %custom-call.62 = f32[1,128,128]{1,2,0:T(8,128)S(1)} custom-call(f32[1,128,128]{2,1,0:T(8,128)S(1)} %get-tuple-element.116), custom_call_target="InvertDiagBlocksLowerTriangular" | custom-call | tf_op jit(solution)/shard_map/jit(cholesky)/cholesky | solution.py:67
  447.3 11.7 %cholesky.506 = f32[128,128]{1,0:T(8,128)S(1)} custom-call(f32[128,128]{1,0:T(8,128)S(1)} %cholesky.599), custom_call_target="Cholesky" | custom-call | tf_op jit(solution)/shard_map/jit(cholesky)/cholesky | solution.py:67
  460.3 9.9 %custom-call.63 = f32[1,128,128]{1,2,0:T(8,128)S(1)} custom-call(f32[1,128,128]{2,1,0:T(8,128)S(1)} %get-tuple-element.113), custom_call_target="InvertDiagBlocksLowerTriangular" | custom-call | tf_op jit(solution)/shard_map/jit(cholesky)/cholesky | solution.py:67
  473.5 11.7 %cholesky.526 = f32[128,128]{1,0:T(8,128)S(1)} custom-call(f32[128,128]{1,0:T(8,128)S(1)} %cholesky.604), custom_call_target="Cholesky" | custom-call | tf_op jit(solution)/shard_map/jit(cholesky)/cholesky | solution.py:67
  486.5 9.8 %custom-call.64 = f32[1,128,128]{1,2,0:T(8,128)S(1)} custom-call(f32[1,128,128]{2,1,0:T(8,128)S(1)} %get-tuple-element.110), custom_call_target="InvertDiagBlocksLowerTriangular" | custom-call | tf_op jit(solution)/shard_map/jit(cholesky)/cholesky | solution.py:67
  499.3 11.9 %cholesky.546 = f32[128,128]{1,0:T(8,128)S(1)} custom-call(f32[128,128]{1,0:T(8,128)S(1)} %cholesky.609), custom_call_target="Cholesky" | custom-call | tf_op jit(solution)/shard_map/jit(cholesky)/cholesky | solution.py:67
  512.5 9.8 %custom-call.65 = f32[1,128,128]{1,2,0:T(8,128)S(1)} custom-call(f32[1,128,128]{2,1,0:T(8,128)S(1)} %get-tuple-element.107), custom_call_target="InvertDiagBlocksLowerTriangular" | custom-call | tf_op jit(solution)/shard_map/jit(cholesky)/cholesky | solution.py:67
  524.9 11.7 %cholesky.564 = f32[128,128]{1,0:T(8,128)S(1)} custom-call(f32[128,128]{1,0:T(8,128)S(1)} %convolution_subtract_fusion.6), custom_call_target="Cholesky" | custom-call | tf_op jit(solution)/shard_map/jit(cholesky)/cholesky | solution.py:67
  (179 shorter events, 100.6 us)
Async XLA Ops:
  58.1 27.8 %all-to-all-start.1 = ((f32[2,512,512]{2,1,0:T(8,128)}), f32[2,512,512]{2,1,0:T(8,128)S(1)}, u32[]{:S(2)}, u32[]{:S(2)}) async-start(f32[2,512,512]{2,1,0:T(8,128)} %copy.19), calls=%async_computation.1 | async-start | bytes 4194304 | tf_op jit(solution)/shard_map/all_to_all | solution.py:24
  87.7 13.0 %copy-start = (s32[8192]{0:T(1024)S(1)}, s32[8192]{0:T(1024)}, u32[]{:S(2)}) copy-start(s32[8192]{0:T(1024)} %param.7) | copy-start | bytes 98308
  93.8 57.6 %all-to-all-start.2 = ((f32[1,512,1024]{2,0,1:T(1,128)}), f32[1,512,1024]{2,0,1:T(1,128)S(1)}, u32[]{:S(2)}, u32[]{:S(2)}) async-start(f32[1,512,1024]{2,0,1:T(1,128)} %copy.21), calls=%async_computation.2 | async-start | bytes 4194304 | tf_op jit(solution)/shard_map/all_to_all | solution.py:42
  100.2 90.1 %all-gather.4.cloned.1.call-start = ((), (), s32[]{:S(2)}) async-start(), calls=%async_computation.4 | async-start | bytes 3145728 | tf_op jit(solution)/shard_map/all_gather | solution.py:55
  156.6 100.1 %reduce-scatter.2.cloned.1.call-start = ((), (), s32[]{:S(2)}) async-start(), calls=%async_computation.5 | async-start | bytes 2228224 | tf_op jit(solution)/shard_map/reduce_scatter | solution.py:60
  194.8 125.5 %all-gather.6.cloned.1.call-start = ((), (), s32[]{:S(2)}) async-start(), calls=%async_computation.6 | async-start | bytes 4325376 | tf_op jit(solution)/shard_map/all_gather | solution.py:61
  338.7 1.9 copy-start.1
Sparse Core Ops, SparseCore 0:
  156.8 33.4 all-gather.3
  195.0 61.7 reduce-scatter.1
  259.7 60.6 all-gather.5
where the time goes:
time: 558 us; the launch traced here: 552 us
  waiting for transfers between devices  183 us (33%)
  other arithmetic  182 us (33%)
  local copies, waits for them, and re-layouts  84.7 us (15%)
  matrix products  43.5 us (8%)
  blocking collectives  28.9 us (5%)
  between operations  18.5 us (3%)
  starting transfers between devices  10.7 us (2%)
    another operation x30, other arithmetic, local(): lower_factor = jnp.linalg.cholesky(gram_matrix)  172 us
    all_gather x1, waiting for transfers between devices, local(): lax.all_gather(gram_block[None], ('row', 'grp'), axis=0, tiled=True)  63.6 us
    reduce_scatter x1, waiting for transfers between devices, local(): lax.psum_scatter(partial_value, 'row', scatter_dimension=0, tiled=True)  61.9 us
    gather x14, local copies, waits for them, and re-layouts, local(): jnp.searchsorted(sample_rows, held_ids)  44 us
    all_gather x1, waiting for transfers between devices, local(): shard_rows = lax.all_gather(sketch_held, 'grp', axis=0, tiled=True)  33.6 us
    all_to_all x1, blocking collectives, local(): lax.all_to_all(local_mix[None], 'grp', split_axis=2, concat_axis=0, tiled...  28.9 us
    all_to_all x1, waiting for transfers between devices, mix_grp(): lax.all_to_all(mix_lead(exchanged), 'grp', split_axis=0, concat_axis=2, t...  23.9 us
    another operation x14, matrix products, local(): lower_factor = jnp.linalg.cholesky(gram_matrix)  23.1 us
  transfers between devices with their start and end apart: 5, of which 4 were waited for; matrix products, arithmetic and copies ran while one was open for 9% of the time, Pallas kernels for 0%

commit v1 on v0

--- a/solution.py
+++ b/solution.py
@@ -32,7 +32,12 @@
     local_table = hadamard(rows_dev, jnp.bfloat16)
     local_mix = jnp.dot(local_table, flipped, preferred_element_type=jnp.float32)
     grp_mixed = mix_grp(
-        lax.all_to_all(local_mix[None], "grp", split_axis=2, concat_axis=0, tiled=True)
+        jnp.concatenate(
+            lax.all_to_all(
+                jnp.stack(jnp.split(local_mix[None], lax.axis_size("grp"), axis=2)), "grp", 0, 0
+            ),
+            axis=0,
+        )
     )
     num_samples = sample_rows.shape[0]
     total_rows = rows_dev * n_row * n_grp

time: 558 us -> 549 us (0.984)
  local copies, waits for them, and re-layouts: 84.7 us -> 77.6 us
where the time goes in v1:
time: 549 us; the launch traced here: 543 us
  waiting for transfers between devices  183 us (33%)
  other arithmetic  182 us (33%)
  local copies, waits for them, and re-layouts  77.6 us (14%)
  matrix products  41.4 us (8%)
  blocking collectives  28.9 us (5%)
  between operations  18.5 us (3%)
  starting transfers between devices  10.7 us (2%)
    another operation x30, other arithmetic, local(): lower_factor = jnp.linalg.cholesky(gram_matrix)  172 us
    all_gather x1, waiting for transfers between devices, local(): lax.all_gather(gram_block[None], ('row', 'grp'), axis=0, tiled=True)  63.5 us
    reduce_scatter x1, waiting for transfers between devices, local(): lax.psum_scatter(partial_value, 'row', scatter_dimension=0, tiled=True)  61.9 us
    gather x14, local copies, waits for them, and re-layouts, local(): jnp.searchsorted(sample_rows, held_ids)  44 us
    all_gather x1, waiting for transfers between devices, local(): shard_rows = lax.all_gather(sketch_held, 'grp', axis=0, tiled=True)  33.6 us
    all_to_all x1, blocking collectives, local(): lax.all_to_all(jnp.stack(jnp.split(local_mix[None], lax.axis_size('grp'),...  28.9 us
    all_to_all x1, waiting for transfers between devices, mix_grp(): lax.all_to_all(mix_lead(exchanged), 'grp', split_axis=0, concat_axis=2, t...  23.9 us
    another operation x14, matrix products, local(): lower_factor = jnp.linalg.cholesky(gram_matrix)  23.1 us
  transfers between devices with their start and end apart: 5, of which 4 were waited for; matrix products, arithmetic and copies ran while one was open for 9% of the time, Pallas kernels for 0%

profile of v1, /device:TPU:0, one launch (start us, length us, event | category | flops | bytes accessed | tf_op | source)
XLA Modules:
  0.0 542.8 jit_solution(16340205755679342012)
XLA Ops:
  10.4 28.9 %all_to_all.35 = f32[2,1,512,512]{3,2,1,0:T(8,128)S(1)} all-to-all(f32[2,1,512,512]{3,2,1,0:T(8,128)S(1)} %pad_maximum_fusion), channel_id=1, replica_groups=mesh['row'=16,'grp'=2] {'grp'}, dimensions={0} | all-to-all | bytes 4194304 | tf_op jit(solution)/shard_map/all_to_all | solution.py:36
  39.3 8.1 %fusion.6 = f32[2,512,512]{2,0,1:T(2,128)S(1)} fusion(f32[2,512,512]{2,1,0:T(8,128)S(1)} %bitcast.74), kind=kOutput, calls=%fused_computation.15 | convolution fusion | flops 12582936 | bytes 4194304 | tf_op jit(solution)/shard_map/ab,bic->aic/dot_general | solution.py:20
  49.2 3.8 all-to-all-start.1
  53.0 23.9 %all-to-all-done.1 = f32[2,512,512]{2,1,0:T(8,128)S(1)} async-done(((f32[2,512,512]{2,1,0:T(8,128)}), f32[2,512,512]{2,1,0:T(8,128)S(1)}, u32[]{:S(2)}, u32[]{:S(2)}) %all-to-all-start.1) | async-done | bytes 2097184 | tf_op jit(solution)/shard_map/all_to_all | solution.py:24
  78.8 6.1 %copy.21 = f32[1,512,1024]{2,0,1:T(1,128)} copy(f32[1,512,1024]{1,2,0:T(8,128)} %bitcast.75) | data formatting | bytes 4194304 | tf_op jit(solution)/shard_map/all_to_all | solution.py:24
  84.9 6.3 %all-to-all-start.2 = ((f32[1,512,1024]{2,0,1:T(1,128)}), f32[1,512,1024]{2,0,1:T(1,128)S(1)}, u32[]{:S(2)}, u32[]{:S(2)}) async-start(f32[1,512,1024]{2,0,1:T(1,128)} %copy.21), calls=%async_computation.2 | async-start | bytes 4194304 | tf_op jit(solution)/shard_map/all_to_all | solution.py:47
  91.8 47.4 %while.24 = (s32[]{:T(128)}, u32[512]{0:T(512)S(1)}, u32[512]{0:T(512)S(1)}, s32[8192]{0:T(1024)S(1)}, s32[16]{0:T(128)S(1)}, /*index=5*/s32[]{:T(128)}, s32[]{:T(128)}, s32[]{}) while((s32[]{:T(128)}, u32[512]{0:T(512)S(1)}, u32[512]{0:T(512)S(1)}, s32[8192]{0:T(1024)S(1)}, s32[16]{0:T(128)S(1)}, /*index=5*/s32[]{:T(128)}, ...), condition=%wide.region_1.2_spmd.clone, body=%wide.region_0.1_spmd.clone.sunk | while | flops 10756 | bytes 46253 | solution.py:56
  91.8 3.1 gather_fusion
  95.2 3.1 gather_fusion
  112.1 3.1 gather_fusion
  147.8 33.6 %all-gather.4.cloned.1.call-done = bf16[1024,1024]{1,0:T(8,128)(2,1)} async-done(((bf16[512,1024]{1,0:T(8,128)(2,1)}), bf16[1024,1024]{1,0:T(8,128)(2,1)}) %all-gather.4.cloned.1.call-update) | async-done | bytes 2097168 | tf_op jit(solution)/shard_map/all_gather | solution.py:60
  181.3 4.5 fusion.12
  186.0 61.9 %reduce-scatter.2.cloned.1.call-done = f32[64,512]{1,0:T(8,128)} async-done(((f32[1024,512]{1,0:T(8,128)}), f32[64,512]{1,0:T(8,128)}) %reduce-scatter.2.cloned.1.call-update) | async-done | bytes 131088 | tf_op jit(solution)/shard_map/reduce_scatter | solution.py:65
  247.8 63.5 %all-gather.6.cloned.1.call-done = f32[2048,512]{1,0:T(8,128)} async-done(((f32[64,512]{1,0:T(8,128)}), f32[2048,512]{1,0:T(8,128)}) %all-gather.6.cloned.1.call-update) | async-done | bytes 4194320 | tf_op jit(solution)/shard_map/all_gather | solution.py:66
  311.4 5.4 %copy.24 = f32[16,2,64,512]{3,1,2,0:T(2,128)S(1)} copy(f32[16,2,64,512]{3,2,1,0:T(8,128)} %bitcast.77) | data formatting | bytes 8388608 | tf_op jit(solution)/shard_map/reshape | solution.py:68
  319.7 5.5 %copy.25 = f32[1024,1024]{0,1:T(8,128)} copy(f32[1024,1024]{1,0:T(8,128)} %bitcast.71) | data formatting | bytes 8388608 | tf_op jit(solution)/shard_map/reshape | solution.py:70
  325.2 4.4 fusion.2
  331.6 11.7 %cholesky.223 = f32[128,128]{1,0:T(8,128)S(1)} custom-call(f32[128,128]{1,0:T(8,128)S(1)} %cholesky.580), custom_call_target="Cholesky" | custom-call | tf_op jit(solution)/shard_map/jit(cholesky)/cholesky | solution.py:72
  343.4 9.8 %custom-call.59 = f32[1,128,128]{1,2,0:T(8,128)S(1)} custom-call(f32[1,128,128]{2,1,0:T(8,128)S(1)} %get-tuple-element.127), custom_call_target="InvertDiagBlocksLowerTriangular" | custom-call | tf_op jit(solution)/shard_map/jit(cholesky)/cholesky | solution.py:72
  359.6 11.9 %cholesky.244 = f32[128,128]{1,0:T(8,128)S(1)} custom-call(f32[128,128]{1,0:T(8,128)S(1)} %cholesky.584), custom_call_target="Cholesky" | custom-call | tf_op jit(solution)/shard_map/jit(cholesky)/cholesky | solution.py:72
  372.2 9.8 %custom-call.60 = f32[1,128,128]{1,2,0:T(8,128)S(1)} custom-call(f32[1,128,128]{2,1,0:T(8,128)S(1)} %get-tuple-element.124), custom_call_target="InvertDiagBlocksLowerTriangular" | custom-call | tf_op jit(solution)/shard_map/jit(cholesky)/cholesky | solution.py:72
  385.3 11.7 %cholesky.468 = f32[128,128]{1,0:T(8,128)S(1)} custom-call(f32[128,128]{1,0:T(8,128)S(1)} %cholesky.589), custom_call_target="Cholesky" | custom-call | tf_op jit(solution)/shard_map/jit(cholesky)/cholesky | solution.py:72
  398.3 9.8 %custom-call.61 = f32[1,128,128]{1,2,0:T(8,128)S(1)} custom-call(f32[1,128,128]{2,1,0:T(8,128)S(1)} %get-tuple-element.121), custom_call_target="InvertDiagBlocksLowerTriangular" | custom-call | tf_op jit(solution)/shard_map/jit(cholesky)/cholesky | solution.py:72
  411.6 12.1 %cholesky.487 = f32[128,128]{1,0:T(8,128)S(1)} custom-call(f32[128,128]{1,0:T(8,128)S(1)} %cholesky.594), custom_call_target="Cholesky" | custom-call | tf_op jit(solution)/shard_map/jit(cholesky)/cholesky | solution.py:72
  425.0 9.8 %custom-call.62 = f32[1,128,128]{1,2,0:T(8,128)S(1)} custom-call(f32[1,128,128]{2,1,0:T(8,128)S(1)} %get-tuple-element.118), custom_call_target="InvertDiagBlocksLowerTriangular" | custom-call | tf_op jit(solution)/shard_map/jit(cholesky)/cholesky | solution.py:72
  438.3 11.7 %cholesky.506 = f32[128,128]{1,0:T(8,128)S(1)} custom-call(f32[128,128]{1,0:T(8,128)S(1)} %cholesky.599), custom_call_target="Cholesky" | custom-call | tf_op jit(solution)/shard_map/jit(cholesky)/cholesky | solution.py:72
  451.3 9.9 %custom-call.63 = f32[1,128,128]{1,2,0:T(8,128)S(1)} custom-call(f32[1,128,128]{2,1,0:T(8,128)S(1)} %get-tuple-element.115), custom_call_target="InvertDiagBlocksLowerTriangular" | custom-call | tf_op jit(solution)/shard_map/jit(cholesky)/cholesky | solution.py:72
  464.5 11.7 %cholesky.526 = f32[128,128]{1,0:T(8,128)S(1)} custom-call(f32[128,128]{1,0:T(8,128)S(1)} %cholesky.604), custom_call_target="Cholesky" | custom-call | tf_op jit(solution)/shard_map/jit(cholesky)/cholesky | solution.py:72
  477.5 9.8 %custom-call.64 = f32[1,128,128]{1,2,0:T(8,128)S(1)} custom-call(f32[1,128,128]{2,1,0:T(8,128)S(1)} %get-tuple-element.112), custom_call_target="InvertDiagBlocksLowerTriangular" | custom-call | tf_op jit(solution)/shard_map/jit(cholesky)/cholesky | solution.py:72
  490.3 11.9 %cholesky.546 = f32[128,128]{1,0:T(8,128)S(1)} custom-call(f32[128,128]{1,0:T(8,128)S(1)} %cholesky.609), custom_call_target="Cholesky" | custom-call | tf_op jit(solution)/shard_map/jit(cholesky)/cholesky | solution.py:72
  503.5 9.8 %custom-call.65 = f32[1,128,128]{1,2,0:T(8,128)S(1)} custom-call(f32[1,128,128]{2,1,0:T(8,128)S(1)} %get-tuple-element.109), custom_call_target="InvertDiagBlocksLowerTriangular" | custom-call | tf_op jit(solution)/shard_map/jit(cholesky)/cholesky | solution.py:72
  515.9 11.7 %cholesky.564 = f32[128,128]{1,0:T(8,128)S(1)} custom-call(f32[128,128]{1,0:T(8,128)S(1)} %convolution_subtract_fusion.6), custom_call_target="Cholesky" | custom-call | tf_op jit(solution)/shard_map/jit(cholesky)/cholesky | solution.py:72
  (178 shorter events, 94.9 us)
Async XLA Ops:
  49.2 27.8 %all-to-all-start.1 = ((f32[2,512,512]{2,1,0:T(8,128)}), f32[2,512,512]{2,1,0:T(8,128)S(1)}, u32[]{:S(2)}, u32[]{:S(2)}) async-start(f32[2,512,512]{2,1,0:T(8,128)} %copy.19), calls=%async_computation.1 | async-start | bytes 4194304 | tf_op jit(solution)/shard_map/all_to_all | solution.py:24
  78.8 13.0 %copy-start = (s32[8192]{0:T(1024)S(1)}, s32[8192]{0:T(1024)}, u32[]{:S(2)}) copy-start(s32[8192]{0:T(1024)} %param.7) | copy-start | bytes 98308
  84.9 57.6 %all-to-all-start.2 = ((f32[1,512,1024]{2,0,1:T(1,128)}), f32[1,512,1024]{2,0,1:T(1,128)S(1)}, u32[]{:S(2)}, u32[]{:S(2)}) async-start(f32[1,512,1024]{2,0,1:T(1,128)} %copy.21), calls=%async_computation.2 | async-start | bytes 4194304 | tf_op jit(solution)/shard_map/all_to_all | solution.py:47
  91.2 90.1 %all-gather.4.cloned.1.call-start = ((), (), s32[]{:S(2)}) async-start(), calls=%async_computation.4 | async-start | bytes 3145728 | tf_op jit(solution)/shard_map/all_gather | solution.py:60
  147.7 100.1 %reduce-scatter.2.cloned.1.call-start = ((), (), s32[]{:S(2)}) async-start(), calls=%async_computation.5 | async-start | bytes 2228224 | tf_op jit(solution)/shard_map/reduce_scatter | solution.py:65
  185.9 125.5 %all-gather.6.cloned.1.call-start = ((), (), s32[]{:S(2)}) async-start(), calls=%async_computation.6 | async-start | bytes 4325376 | tf_op jit(solution)/shard_map/all_gather | solution.py:66
  329.7 1.9 copy-start.1
Sparse Core Ops, SparseCore 0:
  147.8 33.4 all-gather.3
  186.0 61.7 reduce-scatter.1
  250.7 60.6 all-gather.5
